TPU v7x, 256 devices: a whole 4x4x8 slice. The times are simulated.
256 devices in a mesh: pts: 64 (over y, z, core), frq: 4 (over x).
Axes of the slice: x: 4, y: 4, z: 8, core: 2. Of those that a mesh axis runs over, the one named last changes fastest.
Arguments:
- snapshots: bfloat16 [2304, 4, 65536], P('pts', 'frq'), may hold values from -8 to 8
- weights: float32 [4, 65536], P('frq', 'pts'), may hold values from 0.1 to 3
- freq_ids: int32 [65], replicated, may hold values from 0 to 128, as said below
- starts: int32 [16], replicated, may hold values from 0 to 2047, as said below
Outputs:
- mode_field: bfloat16 [65, 2, 16, 4, 65536], P(None, None, None, 'frq', 'pts')
Inputs may be any that keep to these rules, and one draw needn't show every extreme that they name: `freq_ids`: 65 distinct frequency bins of a block of 256 snapshots. Block b starts between b * 128 and b * 128 + 127; the first block starts at 0 and the last at 2047.
All inputs are finite; a program needn't handle non-finite values.
Results may differ from a plain program's by a relative error of at most 0.007.
Values may be sent and summed in bfloat16 or wider, within the bound.
A program may use at most 128 MiB of HBM per device.

v0:
```python
import math

import jax
import jax.numpy as jnp
from jax import lax
from jax.sharding import Mesh
from jax.sharding import PartitionSpec as P

NFFT = 256
ITERS = 3
PTS = ("pts_0", "pts_1", "pts_2")


def split_up(shard, dim, peers):
    shape = shard.shape
    tiles = shard.reshape(*shape[:dim], peers, shape[dim] // peers, *shape[dim + 1 :])
    return jnp.moveaxis(tiles, dim, 0)


def sent_and_summed(shard, axis, dim):
    peers = lax.axis_size(axis)
    tiles = lax.all_to_all(split_up(shard, dim, peers), axis, 0, 0, tiled=True)
    return jnp.sum(tiles, axis=0)


def by_axis(shard, axes):
    for axis in axes:
        shard = lax.psum(shard, axis)
    return shard


def in_order(tiles, dim):
    shape = list(tiles.shape[1:])
    shape[dim] *= tiles.shape[0]
    return jnp.moveaxis(tiles, 0, dim).reshape(shape)


def copy_for_each(shard, axis):
    copies = jnp.broadcast_to(shard, (lax.axis_size(axis), *shard.shape))
    return lax.all_to_all(copies, axis, split_axis=0, concat_axis=0, tiled=True)


def gather_directly(shard, axis, dim):
    return in_order(copy_for_each(shard, axis), dim)


def window_table(freq_ids, length):
    sample_index = jnp.arange(length, dtype=jnp.int32)
    residue = freq_ids[:, None] * sample_index[None, :] % length
    angles = 2.0 * math.pi * residue.astype(jnp.float32) / length
    hann_window = 0.5 - 0.5 * jnp.cos(2.0 * math.pi * sample_index.astype(jnp.float32) / length)
    cos_rows = hann_window[None, :] * jnp.cos(angles)
    sin_rows = -hann_window[None, :] * jnp.sin(angles)
    return jnp.concatenate([cos_rows, sin_rows], axis=0).astype(jnp.bfloat16)


def solve_roots(real_part, imag_part, sweeps):
    order = real_part.shape[1]
    upper_half = jnp.concatenate([real_part, -imag_part], axis=2)
    lower_half = jnp.concatenate([imag_part, real_part], axis=2)
    embed = jnp.concatenate([upper_half, lower_half], axis=1)
    trace_sum = jnp.trace(real_part, axis1=1, axis2=2)
    approx = embed / trace_sum[:, None, None]
    identity = jnp.broadcast_to(jnp.eye(2 * order, dtype=jnp.float32), approx.shape)
    inverse_root = identity
    for iteration in range(sweeps):
        update = 1.5 * identity - 0.5 * jnp.matmul(
            inverse_root, approx, precision=lax.Precision.HIGHEST
        )
        approx = jnp.matmul(approx, update, precision=lax.Precision.HIGHEST)
        inverse_root = jnp.matmul(update, inverse_root, precision=lax.Precision.HIGHEST)
    root_real = inverse_root[:, :order, :order]
    root_imag = inverse_root[:, order:, :order]
    first_rows = jnp.stack([root_real, root_imag], axis=2)
    second_rows = jnp.stack([-root_imag, root_real], axis=2)
    mode_coefs = jnp.stack([first_rows, second_rows], axis=1)
    inv_scale = 1.0 / jnp.sqrt(trace_sum)
    return mode_coefs * inv_scale[:, None, None, None, None]


def shards(snapshots, weights, freq_ids, starts):
    row_count, _, section_points = snapshots.shape
    pieces = lax.axis_size(PTS)
    dev_points = section_points // pieces
    freq_count = freq_ids.shape[0]
    block_total = starts.shape[0]
    total_points = dev_points * pieces * lax.axis_size("frq")
    dft_table = window_table(freq_ids, NFFT)
    columns = lax.all_to_all(
        snapshots.reshape(row_count, pieces, dev_points),
        PTS,
        split_axis=1,
        concat_axis=0,
        tiled=True,
    )[:, 0, :]
    windows = jax.vmap(lambda offset: lax.dynamic_slice_in_dim(columns, offset, NFFT, 0))(starts)
    spectra = jnp.einsum("kt,btn->bkn", dft_table, windows, preferred_element_type=jnp.float32)
    spectra = spectra.astype(jnp.bfloat16).reshape(block_total, 2, freq_count, columns.shape[1])
    point_weight = weights[0]
    weighted = (spectra * point_weight).astype(jnp.bfloat16)
    gram = (
        jnp.einsum("bkfp,clfp->fbkcl", spectra, weighted, preferred_element_type=jnp.float32)
        / total_points
    )
    real_part = gram[:, :, 0, :, 0] + gram[:, :, 1, :, 1]
    imag_part = gram[:, :, 0, :, 1] - gram[:, :, 1, :, 0]
    local_gram = jnp.stack([real_part, imag_part], axis=0)
    groups = lax.axis_size("frq")
    padded = (freq_count + groups - 1) // groups * groups
    local_n = padded // groups
    padded_gram = jnp.pad(local_gram, ((0, 0), (0, padded - freq_count), (0, 0), (0, 0)))
    owned_gram = sent_and_summed(padded_gram, "frq", 1)
    owned_gram = by_axis(owned_gram, PTS)
    owned_index = lax.axis_index("frq") * local_n + jnp.arange(local_n, dtype=jnp.int32)
    filler = (owned_index >= freq_count).astype(jnp.float32)[:, None, None] * jnp.eye(
        block_total, dtype=jnp.float32
    )
    owned_coefs = solve_roots(owned_gram[0] + filler, owned_gram[1], ITERS).astype(jnp.bfloat16)
    mode_coefs = gather_directly(owned_coefs, "frq", 0)[:freq_count]
    mode_field = jnp.einsum(
        "bkfp,fkblm->flmp", spectra, mode_coefs, preferred_element_type=jnp.float32
    )
    mode_field = (mode_field * jnp.sqrt(point_weight)).astype(jnp.bfloat16)
    return mode_field.reshape(freq_count, 2, block_total, 1, dev_points)


def solution(mesh):
    torus = Mesh(
        mesh.devices.reshape(4, 8, 2, mesh.shape["frq"]), ("pts_0", "pts_1", "pts_2", "frq")
    )
    placed = (P(PTS, "frq", None), P("frq", PTS), P(), P())
    return jax.shard_map(
        shards,
        mesh=torus,
        in_specs=placed,
        out_specs=P(None, None, None, "frq", PTS),
        check_vma=False,
    )
```

profile of v0, /device:TPU:1, one launch (start us, length us, event | category | flops | bytes accessed | tf_op | source)
XLA Modules:
  0.0 314.4 jit_solution(3582730954343834698)
XLA Ops:
  0.0 5.5 %copy.82 = bf16[5,8,64,1024]{3,2,1,0:T(8,128)(2,1)S(1)} copy(bf16[5,8,64,1024]{3,1,2,0:T(8,128)(2,1)} %bitcast.96) | data formatting | bytes 10485760
  6.3 4.9 %copy.56 = bf16[36,64,1024]{2,0,1:T(8,128)(2,1)} copy(bf16[36,64,1024]{2,1,0:T(8,128)(2,1)S(1)} %slice.55) | data formatting | bytes 9437184 | tf_op jit(solution)/shard_map/reshape | solution.py:90
  11.3 13.5 %all-to-all-start = ((bf16[36,64,1024]{2,0,1:T(8,128)(2,1)}), bf16[36,64,1024]{2,0,1:T(8,128)(2,1)}, u32[]{:S(2)}, u32[]{:S(2)}) async-start(bf16[36,64,1024]{2,0,1:T(8,128)(2,1)} %copy.56), calls=%async_computation | async-start | bytes 10485760 | tf_op jit(solution)/shard_map/all_to_all | solution.py:89
  25.3 117.8 %all-to-all-done = bf16[36,64,1024]{2,0,1:T(8,128)(2,1)} async-done(((bf16[36,64,1024]{2,0,1:T(8,128)(2,1)}), bf16[36,64,1024]{2,0,1:T(8,128)(2,1)}, u32[]{:S(2)}, u32[]{:S(2)}) %all-to-all-start) | async-done | bytes 4718624 | tf_op jit(solution)/shard_map/all_to_all | solution.py:89
  143.1 7.2 %squeeze.6 = bf16[2304,1024]{1,0:T(8,128)(2,1)} reshape(bf16[64,36,1,1024]{3,1,0,2:T(8,128)(2,1)} %bitcast.1) | data formatting | bytes 9437184 | tf_op jit(solution)/shard_map/squeeze | solution.py:89
  150.3 51.4 %while.1 = (s32[]{:T(128)}, bf16[2304,1024]{1,0:T(8,128)(2,1)}, s32[16,2]{0,1:T(2,128)S(1)}, bf16[16,256,1024]{2,1,0:T(8,128)(2,1)}, s32[]{:T(128)}) while((s32[]{:T(128)}, bf16[2304,1024]{1,0:T(8,128)(2,1)}, s32[16,2]{0,1:T(2,128)S(1)}, bf16[16,256,1024]{2,1,0:T(8,128)(2,1)}, s32[]{:T(128)}) %tuple.24), condition=%wide.while_cond, body=%wide.while_body.sunk | while | flops 2 | bytes 1049189 | solution.py:96
  154.1 2.6 bitcast_dynamic-update-slice_fusion.2
  157.3 2.6 bitcast_dynamic-update-slice_fusion.2
  160.5 2.6 bitcast_dynamic-update-slice_fusion.2
  173.4 2.6 bitcast_dynamic-update-slice_fusion.2
  179.8 2.6 bitcast_dynamic-update-slice_fusion.2
  192.7 2.6 bitcast_dynamic-update-slice_fusion.2
  199.1 2.6 bitcast_dynamic-update-slice_fusion.2
  201.7 6.3 %convert_bitcast_fusion = bf16[16,130,1024]{2,1,0:T(8,128)(2,1)S(1)} fusion(bf16[16,256,1024]{2,1,0:T(8,128)(2,1)} %get-tuple-element.12, bf16[65,256]{1,0:T(8,128)(2,1)S(1)} %get-tuple-element.31, bf16[65,256]{1,0:T(8,128)(2,1)S(1)} %get-tuple-element.30), kind=kOutput, calls=%fused_computation.5 | convolution fusion | flops 1092782080 | bytes 12715008 | tf_op jit(solution)/shard_map/kt,btn->bkn/dot_general | solution.py:97
  210.5 6.3 %fusion.10 = f32[65,16,2,16,2]{3,1,4,2,0:T(8,128)S(1)} fusion(bf16[16,2,65,1024,1]{3,0,2,1,4:T(8,128)(2,1)S(1)} %bitcast.97, bf16[16,2,65,1024]{3,0,2,1:T(8,128)(2,1)S(1)} %bitcast.98, f32[1024]{0:T(1024)S(1)} %bitcast.106), kind=kOutput, calls=%fused_computation.13 | convolution fusion | flops 142771200 | bytes 8790016 | tf_op jit(solution)/shard_map/bkfp,clfp->fbkcl/dot_general | solution.py:102
  219.5 4.0 %all-to-all-start.1 = ((f32[4,1,8704]{2,1,0:T(1,128)}), f32[4,1,8704]{2,1,0:T(1,128)S(1)}, u32[]{:S(2)}, u32[]{:S(2)}) async-start(f32[4,1,8704]{2,1,0:T(1,128)} %reshape.118), calls=%async_computation.1 | async-start | bytes 278528 | tf_op jit(solution)/shard_map/all_to_all | solution.py:22
  223.6 4.9 %all-to-all-done.1 = f32[4,1,8704]{2,1,0:T(1,128)S(1)} async-done(((f32[4,1,8704]{2,1,0:T(1,128)}), f32[4,1,8704]{2,1,0:T(1,128)S(1)}, u32[]{:S(2)}, u32[]{:S(2)}) %all-to-all-start.1) | async-done | bytes 139296 | tf_op jit(solution)/shard_map/all_to_all | solution.py:22
  231.3 16.5 %psum.21 = f32[2,17,16,16]{3,2,1,0:T(8,128)S(1)} all-reduce(f32[2,17,16,16]{3,2,1,0:T(8,128)S(1)} %copy.63), channel_id=1, replica_groups=mesh['pts_0'=4,'pts_1'=8,'pts_2'=2,'frq'=4] {'pts_0'}, use_global_device_ids=true, to_apply=%region_1.2 | all-reduce | flops 8704 | bytes 69632 | tf_op jit(solution)/shard_map/psum | solution.py:28
  247.8 23.7 %psum.22 = f32[2,17,16,16]{3,2,1,0:T(8,128)S(1)} all-reduce(f32[2,17,16,16]{3,2,1,0:T(8,128)S(1)} %psum.21), channel_id=1, replica_groups=mesh['pts_0'=4,'pts_1'=8,'pts_2'=2,'frq'=4] {'pts_1'}, use_global_device_ids=true, to_apply=%region_2.3 | all-reduce | flops 8704 | bytes 69632 | tf_op jit(solution)/shard_map/psum | solution.py:28
  271.5 15.9 %psum.23 = f32[2,17,16,16]{3,2,1,0:T(8,128)S(1)} all-reduce(f32[2,17,16,16]{3,2,1,0:T(8,128)S(1)} %psum.22), channel_id=1, replica_groups=mesh['pts_0'=4,'pts_1'=8,'pts_2'=2,'frq'=4] {'pts_2'}, use_global_device_ids=true, to_apply=%region_3.4 | all-reduce | flops 8704 | bytes 69632 | tf_op jit(solution)/shard_map/psum | solution.py:28
  294.2 3.6 %all-to-all-start.2 = ((bf16[4,2,8704]{2,1,0:T(2,128)(2,1)}), bf16[4,2,8704]{2,1,0:T(2,128)(2,1)S(1)}, u32[]{:S(2)}, u32[]{:S(2)}) async-start(bf16[4,2,8704]{2,1,0:T(2,128)(2,1)} %reshape.120), calls=%async_computation.2 | async-start | bytes 278528 | tf_op jit(solution)/shard_map/all_to_all | solution.py:40
  297.8 4.7 %all-to-all-done.2 = bf16[4,2,8704]{2,1,0:T(2,128)(2,1)S(1)} async-done(((bf16[4,2,8704]{2,1,0:T(2,128)(2,1)}), bf16[4,2,8704]{2,1,0:T(2,128)(2,1)S(1)}, u32[]{:S(2)}, u32[]{:S(2)}) %all-to-all-start.2) | async-done | bytes 139296 | tf_op jit(solution)/shard_map/all_to_all | solution.py:40
  305.0 2.7 copy.67
  307.8 6.6 %fusion.2 = bf16[65,2,16,1,1024]{4,2,3,1,0:T(8,128)(2,1)} fusion(f32[1024]{0:T(1024)S(1)} %sqrt.11, bf16[68,2,16,2,16]{2,4,1,3,0:T(8,128)(2,1)S(1)} %bitcast.104, bf16[16,2,65,1024,1]{3,0,2,1,4:T(8,128)(2,1)} %bitcast.99), kind=kOutput, calls=%fused_computation.7 | convolution fusion | flops 140574720 | bytes 8663040 | tf_op jit(solution)/shard_map/bkfp,fkblm->flmp/dot_general | solution.py:120
  (93 shorter events, 51.4 us)
Async XLA Ops:
  11.3 13.5 %copy-start.3 = (s32[16]{0:T(128)S(1)}, s32[16]{0:T(128)}, u32[]{:S(2)}) copy-start(s32[16]{0:T(128)} %param.7) | copy-start | bytes 196
  11.3 13.6 %copy-start.2 = (s32[65]{0:T(128)S(1)}, s32[65]{0:T(128)}, u32[]{:S(2)}) copy-start(s32[65]{0:T(128)} %param.6) | copy-start | bytes 784
  11.3 131.8 %all-to-all-start = ((bf16[36,64,1024]{2,0,1:T(8,128)(2,1)}), bf16[36,64,1024]{2,0,1:T(8,128)(2,1)}, u32[]{:S(2)}, u32[]{:S(2)}) async-start(bf16[36,64,1024]{2,0,1:T(8,128)(2,1)} %copy.56), calls=%async_computation | async-start | bytes 10485760 | tf_op jit(solution)/shard_map/all_to_all | solution.py:89
  208.1 2.4 copy-start.1
  210.4 6.3 %copy-start = (bf16[16,130,1024]{2,0,1:T(8,128)(2,1)}, bf16[16,130,1024]{2,0,1:T(8,128)(2,1)S(1)}, u32[]{:S(2)}) copy-start(bf16[16,130,1024]{2,0,1:T(8,128)(2,1)S(1)} %copy.57) | copy-start | bytes 12779524
  219.5 8.9 %all-to-all-start.1 = ((f32[4,1,8704]{2,1,0:T(1,128)}), f32[4,1,8704]{2,1,0:T(1,128)S(1)}, u32[]{:S(2)}, u32[]{:S(2)}) async-start(f32[4,1,8704]{2,1,0:T(1,128)} %reshape.118), calls=%async_computation.1 | async-start | bytes 278528 | tf_op jit(solution)/shard_map/all_to_all | solution.py:22
  294.2 8.3 %all-to-all-start.2 = ((bf16[4,2,8704]{2,1,0:T(2,128)(2,1)}), bf16[4,2,8704]{2,1,0:T(2,128)(2,1)S(1)}, u32[]{:S(2)}, u32[]{:S(2)}) async-start(bf16[4,2,8704]{2,1,0:T(2,128)(2,1)} %reshape.120), calls=%async_computation.2 | async-start | bytes 278528 | tf_op jit(solution)/shard_map/all_to_all | solution.py:40
where the time goes:
time: 316 us; the launch traced here: 314 us
  waiting for transfers between devices  127 us (40%)
  local copies, waits for them, and re-layouts  84.7 us (27%)
  blocking collectives  56.2 us (18%)
  matrix products  22.6 us (7%)
  starting transfers between devices  21.1 us (7%)
    all_to_all x1, waiting for transfers between devices, shards(): lax.all_to_all(snapshots.reshape(row_count, pieces, dev_points), PTS, spl...  118 us
    psum x3, blocking collectives, by_axis(): shard = lax.psum(shard, axis)  56.2 us
    gather x48, local copies, waits for them, and re-layouts  51.4 us
    all_to_all x1, starting transfers between devices, shards(): lax.all_to_all(snapshots.reshape(row_count, pieces, dev_points), PTS, spl...  13.5 us
    unnamed x16, local copies, waits for them, and re-layouts  13.3 us
    squeeze x1, local copies, waits for them, and re-layouts, shards(): lax.all_to_all(snapshots.reshape(row_count, pieces, dev_points), PTS, spl...  7.23 us
    dot_general x1, matrix products, shards(): jnp.einsum('bkfp,fkblm->flmp', spectra, mode_coefs, preferred_element_typ...  6.59 us
    dot_general x1, matrix products, shards(): jnp.einsum('kt,btn->bkn', dft_table, windows, preferred_element_type=jnp....  6.34 us
  transfers between devices with their start and end apart: 3, of which 3 were waited for; matrix products, arithmetic and copies ran while one was open for 0% of the time, Pallas kernels for 0%

commit v1 on v0

v1 whole, which is shorter than its diff:
```python
import functools
import math

import jax
import jax.numpy as jnp
from jax import lax
from jax.experimental import pallas as pl
from jax.experimental.pallas import tpu as pltpu
from jax.sharding import Mesh
from jax.sharding import PartitionSpec as P

NFFT = 256
ITERS = 3
PTS = ("pts_0", "pts_1", "pts_2")
NY, NZ, NC, NX = 4, 8, 2, 4
PEERS = NY * NZ * NC
ROWS = 36
MAIN = 32
REST = ROWS - MAIN
BLOCKS = 16
FREQS = 65
GROUP = 8
GROUPS = 9
SIDE = BLOCKS * GROUP * 2
TROWS = GROUPS * GROUP * 2
POINTS = 1024
CHUNKS = 4
W = POINTS // CHUNKS
HALF = W // 2
KMAIN = 12 * MAIN
KREST = 64
TOTAL = 262144
MESH = pl.DeviceIdType.MESH
F32 = jnp.float32
BF16 = jnp.bfloat16
HIGH = lax.Precision.HIGHEST
NT = (((1,), (1,)), ((), ()))


def iota(shape, dim):
    return lax.broadcasted_iota(jnp.int32, shape, dim)


def first_source(b):
    return min(128 * b // ROWS, PEERS - 12)


def first_rest(b):
    return min(REST * first_source(b) // 16 * 16, PEERS * REST - KREST)


def same_frequency():
    return (iota((SIDE, SIDE), 0) // 2) % GROUP == (iota((SIDE, SIDE), 1) // 2) % GROUP


def spread():
    row, col = iota((SIDE, 2 * BLOCKS), 0), iota((SIDE, 2 * BLOCKS), 1)
    return (col % BLOCKS == row // (2 * GROUP)) & (col // BLOCKS == row % 2)


def first_part(shape):
    return iota(shape, len(shape) - 1) % 2 == 0


def sum_frequencies(m):
    m = m.reshape(BLOCKS, 2 * GROUP, SIDE)
    m = m[:, :8, :] + m[:, 8:, :]
    m = m + pltpu.roll(m, 4, 1)
    return m + pltpu.roll(m, 2, 1)


def first_rows(m, h3):
    m = m.reshape(BLOCKS * 8, SIDE)
    for half in range(2):
        h3[half] = m[:, 128 * half : 128 * half + 128]
    return jnp.concatenate([h3[half, pl.ds(0, BLOCKS, stride=8), :] for half in range(2)], axis=1)


def make_table(fid):
    row = iota((TROWS, FREQS), 0) // 2
    freq = jnp.sum(
        jnp.where(row == iota((TROWS, FREQS), 1), fid.astype(F32), 0.0), axis=1, keepdims=True
    ).astype(jnp.int32)
    t = iota((TROWS, NFFT), 1)
    r = iota((TROWS, NFFT), 0)
    residue = (freq * t + 64 * (r % 2)) % NFFT
    hann = 0.5 - 0.5 * jnp.cos(2.0 * math.pi * t.astype(F32) / NFFT)
    table = hann * jnp.cos(2.0 * math.pi * residue.astype(F32) / NFFT)
    return jnp.where(r // 2 < FREQS, table, 0.0).astype(BF16)


def column_times(b):
    col = iota((1, KMAIN + KREST), 1)
    main = ROWS * (first_source(b) + col // MAIN) + col % MAIN
    rest = col - KMAIN
    rest = ROWS * (first_rest(b) // REST + rest // REST) + MAIN + rest % REST
    return jnp.where(col < KMAIN, main, rest)


def solve_roots(h, group, h3):
    lane = iota((1, SIDE), 1)
    even = lane % 2 == 0
    diag = (iota((BLOCKS, SIDE), 0) == iota((BLOCKS, SIDE), 1) // (2 * GROUP)) & even
    trace = jnp.sum(jnp.where(diag, h, 0.0), axis=0, keepdims=True)
    trace = jnp.broadcast_to(trace, (8, SIDE))
    for step in (16, 32, 64, 128):
        trace = trace + pltpu.roll(trace, step, 1)
    trace = (trace + pltpu.roll(trace, 1, 1))[:1]
    trace = jnp.where(group * GROUP + (lane // 2) % GROUP < FREQS, trace, 1.0)
    rows = jnp.concatenate(
        [
            jnp.where(even, h, -h),
            jnp.where(even, pltpu.roll(h, SIDE - 1, 1), pltpu.roll(h, 1, 1)),
        ],
        axis=0,
    )
    mask = same_frequency()
    dot = functools.partial(jnp.dot, precision=HIGH, preferred_element_type=F32)
    approx = jnp.where(mask, dot(spread().astype(F32), rows / trace), 0.0)
    eye = jnp.where(iota((SIDE, SIDE), 0) == iota((SIDE, SIDE), 1), 1.5, 0.0)
    update = eye - 0.5 * approx
    root = update
    for _ in range(1, ITERS):
        approx = dot(approx, update)
        update = eye - 0.5 * dot(root, approx)
        root = dot(update, root)
    return (first_rows(sum_frequencies(root), h3) * (1.0 / jnp.sqrt(trace))).astype(BF16)


def spectra_kernel(
    x, w, fid, starts, s_out, hc,
    xs, pk, xm, xr, xu, tab, spec, gram, hsend, r1, h2, r2, hcs, h3,
    in_sem, own_main, own_rest, send_main, send_rest, recv_main, recv_rest, out_sem,
    s1_send, s1_recv, s2_send, s2_recv, s3_send, s3_recv,
):
    y, z, c = (lax.axis_index(a) for a in PTS)
    xx = lax.axis_index("frq")
    me = (y * NZ + z) * NC + c
    load = pltpu.make_async_copy(x, xs, in_sem)
    load.start()

    def at(dx, dy, dz, dc):
        return {
            "pts_0": (y + dy) % NY, "pts_1": (z + dz) % NZ, "pts_2": (c + dc) % NC,
            "frq": (xx + dx) % NX,
        }

    def plane(k):
        j, dy, dc = k % 8, (k // 8) % 4, k // 32
        dz = (1 - j % 2) * (j // 2) + (j % 2) * (8 - (j + 1) // 2)
        return at(0, dy, dz, dc)

    barrier = pltpu.get_barrier_semaphore()

    def greet(k, carry):
        pl.semaphore_signal(barrier, inc=1, device_id=plane(k), device_id_type=MESH)
        return carry

    def greet_far(k, carry):
        pl.semaphore_signal(
            barrier, inc=1, device_id=at(1 + k // 4, k % 4, 0, 0), device_id_type=MESH
        )
        return carry

    lax.fori_loop(1, PEERS, greet, 0)
    lax.fori_loop(0, 12, greet_far, 0)
    load.wait()

    low = iota((8, HALF), 0) < 4

    def pack(q, carry):
        for ch in range(CHUNKS):
            left = xs[MAIN:ROWS, pl.ds(pl.multiple_of(q * POINTS + ch * W, 128), HALF)]
            right = xs[MAIN:ROWS, pl.ds(pl.multiple_of(q * POINTS + ch * W + HALF, 128), HALF)]
            pk[q, ch] = jnp.concatenate([left.astype(F32), right.astype(F32)], axis=0).astype(BF16)
        return carry

    lax.fori_loop(0, PEERS, pack, 0)
    pl.semaphore_wait(barrier, PEERS - 1 + 12)

    for ch in range(CHUNKS):
        pltpu.make_async_copy(
            xs.at[0:MAIN, pl.ds(pl.multiple_of(me * POINTS + ch * W, 128), W)],
            xm.at[ch, pl.ds(pl.multiple_of(me * MAIN, MAIN), MAIN), :],
            own_main.at[ch],
        ).start()
        pltpu.make_async_copy(pk.at[me, ch], xr.at[ch, me], own_rest.at[ch]).start()

        def send(k, carry):
            to = plane(k)
            q = (to["pts_0"] * NZ + to["pts_1"]) * NC + to["pts_2"]
            pltpu.make_async_remote_copy(
                src_ref=xs.at[0:MAIN, pl.ds(pl.multiple_of(q * POINTS + ch * W, 128), W)],
                dst_ref=xm.at[ch, pl.ds(pl.multiple_of(me * MAIN, MAIN), MAIN), :],
                send_sem=send_main.at[ch], recv_sem=recv_main.at[ch],
                device_id=to, device_id_type=MESH,
            ).start()
            pltpu.make_async_remote_copy(
                src_ref=pk.at[q, ch], dst_ref=xr.at[ch, me],
                send_sem=send_rest.at[ch], recv_sem=recv_rest.at[ch],
                device_id=to, device_id_type=MESH,
            ).start()
            return carry

        lax.fori_loop(1, PEERS, send, 0)

    table = make_table(fid[...])
    tau = iota((NFFT, KMAIN + KREST), 0)
    for b in range(BLOCKS):
        pick = jnp.where(tau == column_times(b) - starts[b], 1.0, 0.0).astype(BF16)
        tab[b] = jnp.dot(table, pick, preferred_element_type=F32).astype(BF16)

    def finished(ref, sem):
        pltpu.make_async_copy(ref, ref, sem).wait()

    gram[...] = jnp.zeros_like(gram)

    def chunk(ch, carry):
        finished(xm.at[ch, pl.ds(0, MAIN), :], own_main.at[ch])
        finished(xr.at[ch, 0], own_rest.at[ch])
        finished(xm.at[ch, pl.ds(0, (PEERS - 1) * MAIN), :], recv_main.at[ch])
        finished(xr.at[ch, pl.ds(0, PEERS - 1)], recv_rest.at[ch])
        rest = xr[ch].astype(F32).reshape(PEERS // 2, 2, 8, HALF)
        first, second = rest[:, 0], rest[:, 1]
        top = iota((PEERS // 2, 8, HALF), 1) < 4
        left = jnp.where(top, first, pltpu.roll(second, 4, 1))
        right = jnp.where(top, pltpu.roll(first, 4, 1), second)
        xu[:, :HALF] = left.reshape(PEERS * REST, HALF).astype(BF16)
        xu[:, HALF:] = right.reshape(PEERS * REST, HALF).astype(BF16)
        for b in range(BLOCKS):
            s0, r0 = MAIN * first_source(b), first_rest(b)
            part = jnp.concatenate([xm[ch, s0 : s0 + KMAIN, :], xu[r0 : r0 + KREST, :]], axis=0)
            rows = jnp.dot(tab[b], part, preferred_element_type=F32).astype(BF16)
            for g in range(GROUPS):
                spec[ch, g, 16 * b : 16 * b + 16, :] = rows[16 * g : 16 * g + 16, :]
        weight = w[:, pl.ds(pl.multiple_of(ch * W, W), W)]
        for g in range(GROUPS):
            s = spec[ch, g]
            weighted = (s.astype(F32) * weight).astype(BF16)
            gram[g] += lax.dot_general(s, weighted, NT, preferred_element_type=F32)
        pltpu.make_async_copy(
            spec.at[ch], s_out.at[:, :, pl.ds(pl.multiple_of(ch * W, W), W)], out_sem.at[ch]
        ).start()
        return carry

    lax.fori_loop(0, CHUNKS, chunk, 0)

    mask = same_frequency()
    even3 = first_part((BLOCKS, 8, SIDE))
    for g in range(GROUPS):
        m = sum_frequencies(jnp.where(mask, gram[g], 0.0))
        other = pltpu.roll(m, 7, 1)
        m = jnp.where(even3, m + pltpu.roll(other, SIDE - 1, 2), m - pltpu.roll(other, 1, 2))
        hsend[g] = first_rows(m, h3.at[g % 2]) * (1.0 / TOTAL)

    mine = jnp.where(c == 0, z, GROUPS - 1)
    owner = (c == 0) | (z == 0)
    here = z * NC + c

    def stage1(g):
        oz, oc = (g, 0) if g < NZ else (0, 1)
        return pltpu.make_async_remote_copy(
            src_ref=hsend.at[g], dst_ref=r1.at[here], send_sem=s1_send.at[g], recv_sem=s1_recv,
            device_id={"pts_0": y, "pts_1": oz, "pts_2": oc, "frq": xx}, device_id_type=MESH,
        )

    def elsewhere(g):
        return (z != g) | (c != 0) if g < NZ else (z != 0) | (c != 1)

    for g in range(GROUPS):
        @pl.when(elsewhere(g))
        def _():
            stage1(g).start()

    def stage2(k):
        return pltpu.make_async_remote_copy(
            src_ref=h2, dst_ref=r2.at[xx * NY + y], send_sem=s2_send, recv_sem=s2_recv,
            device_id=at(k // 4, k % 4, 0, 0), device_id_type=MESH,
        )

    def stage3(k):
        return pltpu.make_async_remote_copy(
            src_ref=hcs, dst_ref=hc.at[mine], send_sem=s3_send, recv_sem=s3_recv.at[mine],
            device_id=at(0, 0, k // 2, k % 2), device_id_type=MESH,
        )

    @pl.when(owner)
    def _():
        r1[here] = hsend[mine]
        finished(r1.at[pl.ds(0, 15)], s1_recv)
        total = r1[0]
        for i in range(1, 16):
            total = total + r1[i]
        h2[...] = total
        r2[xx * NY + y] = total

        def out2(k, carry):
            stage2(k).start()
            return carry

        lax.fori_loop(1, 16, out2, 0)
        finished(r2.at[pl.ds(0, 15)], s2_recv)
        total = r2[0]
        for i in range(1, 16):
            total = total + r2[i]
        coefs = solve_roots(total, mine, h3.at[0])
        hcs[...] = coefs
        hc[mine] = coefs

        def out3(k, carry):
            stage3(k).start()
            return carry

        lax.fori_loop(1, 16, out3, 0)
        finished(r2.at[pl.ds(0, 15)], s2_send)

    for g in range(GROUPS):
        @pl.when(elsewhere(g))
        def _():
            stage1(g).wait_send()
            finished(hc.at[g], s3_recv.at[g])

    @pl.when(owner)
    def _():
        finished(xm.at[0, pl.ds(0, 15 * BLOCKS), :], s3_send)

    for ch in range(CHUNKS):
        finished(xm.at[ch, pl.ds(0, (PEERS - 1) * MAIN), :], send_main.at[ch])
        finished(xr.at[ch, pl.ds(0, PEERS - 1)], send_rest.at[ch])
        pltpu.make_async_copy(
            spec.at[ch], s_out.at[:, :, pl.ds(ch * W, W)], out_sem.at[ch]
        ).wait()


def project_kernel(hc, s, w, out):
    h = hc[0].astype(F32)
    even = first_part((1, SIDE))
    rows = jnp.concatenate(
        [
            jnp.where(even, h, -h),
            jnp.where(even, pltpu.roll(h, SIDE - 1, 1), pltpu.roll(h, 1, 1)),
        ],
        axis=0,
    ).astype(BF16)
    coefs = jnp.dot(spread().astype(F32).astype(BF16), rows, preferred_element_type=F32)
    coefs = jnp.where(same_frequency(), coefs, 0.0).astype(BF16)
    row, col = iota((SIDE, SIDE), 0), iota((SIDE, SIDE), 1)
    order = jnp.where(
        col == (row % 16) * 16 + (row // 32) * 2 + (row // 16) % 2, 1.0, 0.0
    ).astype(BF16)
    matrix = lax.dot_general(order, coefs, NT, preferred_element_type=F32).astype(BF16)
    field = jnp.dot(matrix, s[0], preferred_element_type=F32)
    out[...] = (field * jnp.sqrt(w[...])).astype(BF16)


def shards(snapshots, weights, freq_ids, starts):
    vmem = pl.BlockSpec(memory_space=pltpu.VMEM)
    anywhere = pl.BlockSpec(memory_space=pl.ANY)
    dma = pltpu.SemaphoreType.DMA
    spectra, coefs = pl.pallas_call(
        spectra_kernel,
        name="exchange_spectra",
        out_shape=(
            jax.ShapeDtypeStruct((GROUPS, SIDE, POINTS), BF16),
            jax.ShapeDtypeStruct((GROUPS, BLOCKS, SIDE), BF16),
        ),
        in_specs=[anywhere, vmem, vmem, pl.BlockSpec(memory_space=pltpu.SMEM)],
        out_specs=(anywhere, vmem),
        scratch_shapes=[
            pltpu.VMEM((ROWS, PEERS * POINTS), BF16),
            pltpu.VMEM((PEERS, CHUNKS, 8, HALF), BF16),
            pltpu.VMEM((CHUNKS, PEERS * MAIN, W), BF16),
            pltpu.VMEM((CHUNKS, PEERS, 8, HALF), BF16),
            pltpu.VMEM((PEERS * REST, W), BF16),
            pltpu.VMEM((BLOCKS, TROWS, KMAIN + KREST), BF16),
            pltpu.VMEM((CHUNKS, GROUPS, SIDE, W), BF16),
            pltpu.VMEM((GROUPS, SIDE, SIDE), F32),
            pltpu.VMEM((GROUPS, BLOCKS, SIDE), F32),
            pltpu.VMEM((16, BLOCKS, SIDE), F32),
            pltpu.VMEM((BLOCKS, SIDE), F32),
            pltpu.VMEM((16, BLOCKS, SIDE), F32),
            pltpu.VMEM((BLOCKS, SIDE), BF16),
            pltpu.VMEM((2, 2, BLOCKS * 8, 128), F32),
            dma(()), dma((CHUNKS,)), dma((CHUNKS,)), dma((CHUNKS,)), dma((CHUNKS,)),
            dma((CHUNKS,)), dma((CHUNKS,)), dma((CHUNKS,)),
            dma((GROUPS,)), dma(()), dma(()), dma(()), dma(()), dma((GROUPS,)),
        ],
        compiler_params=pltpu.CompilerParams(
            collective_id=0, has_side_effects=True, vmem_limit_bytes=56 << 20
        ),
    )(snapshots.reshape(ROWS, PEERS * POINTS), weights, freq_ids.reshape(1, FREQS), starts)
    field = pl.pallas_call(
        project_kernel,
        name="project_modes",
        grid=(GROUPS,),
        out_shape=jax.ShapeDtypeStruct((FREQS * 2 * BLOCKS, POINTS), BF16),
        in_specs=[
            pl.BlockSpec((1, BLOCKS, SIDE), lambda g: (g, 0, 0)),
            pl.BlockSpec((1, SIDE, POINTS), lambda g: (g, 0, 0)),
            pl.BlockSpec((1, POINTS), lambda g: (0, 0)),
        ],
        out_specs=pl.BlockSpec((SIDE, POINTS), lambda g: (g, 0)),
    )(coefs, spectra, weights)
    return field.reshape(FREQS, 2, BLOCKS, 1, POINTS)


def solution(mesh):
    torus = Mesh(
        mesh.devices.reshape(NY, NZ, NC, mesh.shape["frq"]), ("pts_0", "pts_1", "pts_2", "frq")
    )
    placed = (P(PTS, "frq", None), P("frq", PTS), P(), P())
    return jax.shard_map(
        shards,
        mesh=torus,
        in_specs=placed,
        out_specs=P(None, None, None, "frq", PTS),
        check_vma=False,
    )
```

time: 316 us -> 155 us (0.49)
  Pallas kernels: 0 us -> 155 us
  waiting for transfers between devices: 127 us -> 0 us
  local copies, waits for them, and re-layouts: 84.7 us -> 0 us
  blocking collectives: 56.2 us -> 0 us
  matrix products: 22.6 us -> 0 us
  starting transfers between devices: 21.1 us -> 0 us
    pallas_call x0 -> x2, Pallas kernels: none -> 155 us  [the longest x1 145 us: shards(): pl.pallas_call(spectra_kernel, name='exchange_spectra', out_shape=(jax.Sh...]
    all_to_all x3 -> x0, waiting for transfers between devices: 127 us -> none  [the longest x1 118 us: shards(): lax.all_to_all(snapshots.reshape(row_count, pieces, dev_points), PTS, spl...]
    psum x3 -> x0, blocking collectives: 56.2 us -> none  [by_axis(): shard = lax.psum(shard, axis)]
    gather x48 -> x0, local copies, waits for them, and re-layouts: 51.4 us -> none
    dot_general x11 -> x0, matrix products: 22.6 us -> none  [the longest x1 6.59 us: shards(): jnp.einsum('bkfp,fkblm->flmp', spectra, mode_coefs, preferred_element_typ...]
    all_to_all x3 -> x0, starting transfers between devices: 21.1 us -> none  [the longest x1 13.5 us: shards(): lax.all_to_all(snapshots.reshape(row_count, pieces, dev_points), PTS, spl...]
    unnamed x16 -> x0, local copies, waits for them, and re-layouts: 13.3 us -> none
    squeeze x2 -> x0, local copies, waits for them, and re-layouts: 7.24 us -> none  [the longest x1 7.23 us: shards(): lax.all_to_all(snapshots.reshape(row_count, pieces, dev_points), PTS, spl...]
  transfers between devices with their start and end apart: 3 -> 0, of which waited for: 3 -> 0; matrix products, arithmetic and copies ran while one was open for 0% -> 0% of each run, Pallas kernels for 0% -> 0%
where the time goes in v1:
time: 155 us
  Pallas kernels  155 us (100%)
    pallas_call x1, Pallas kernels, shards(): pl.pallas_call(spectra_kernel, name='exchange_spectra', out_shape=(jax.Sh...  145 us
    pallas_call x1, Pallas kernels, shards(): pl.pallas_call(project_kernel, name='project_modes', grid=(GROUPS,), out_...  10.1 us

profile of v1, /device:TPU:1, one launch (start us, length us, event | category | flops | bytes accessed | tf_op | source)
XLA Modules:
  0.0 154.7 jit_solution(878432268840277149)
XLA Ops:
  0.0 144.5 %exchange_spectra.1 = (bf16[9,256,1024]{2,1,0:T(8,128)(2,1)}, bf16[9,16,256]{2,1,0:T(8,128)(2,1)}) custom-call(bf16[36,65536]{1,0:T(8,128)(2,1)} %bitcast.5, f32[1,1024]{1,0:T(1,128)} %w.3, s32[1,65]{1,0:T(1,128)} %bitcast.6, s32[16]{0:T(128)} %starts.1), custom_call_target="tpu_custom_call" | custom-call | tf_op jit(solution)/shard_map/exchange_spectra/pallas_call | solution.py:360
  144.5 10.1 %project_modes.1 = bf16[2080,1024]{1,0:T(8,128)(2,1)} custom-call(bf16[9,16,256]{2,1,0:T(8,128)(2,1)} %get-tuple-element.7.hc, bf16[9,256,1024]{2,1,0:T(8,128)(2,1)} %get-tuple-element.8.s, f32[1,1024]{1,0:T(1,128)} %w.3), custom_call_target="tpu_custom_call" | custom-call | tf_op jit(solution)/shard_map/project_modes/pallas_call | solution.py:392

commit v2 on v1

--- a/solution.py
+++ b/solution.py
@@ -128,9 +128,9 @@
 
 
 def spectra_kernel(
-    x, w, fid, starts, s_out, hc,
-    xs, pk, xm, xr, xu, tab, spec, gram, hsend, r1, h2, r2, hcs, h3,
-    in_sem, own_main, own_rest, send_main, send_rest, recv_main, recv_rest, out_sem,
+    x, w, fid, starts, spec, hc,
+    xs, pk, xm, xr, xu, tab, gram, hsend, r1, h2, r2, hcs, h3,
+    in_sem, own_main, own_rest, send_main, send_rest, recv_main, recv_rest,
     s1_send, s1_recv, s2_send, s2_recv, s3_send, s3_recv,
 ):
     y, z, c = (lax.axis_index(a) for a in PTS)
@@ -162,8 +162,10 @@
         )
         return carry
 
-    lax.fori_loop(1, PEERS, greet, 0)
-    lax.fori_loop(0, 12, greet_far, 0)
+    for k in range(12):
+        greet_far(k, 0)
+    for k in range(PEERS - 1, 0, -1):
+        greet(k, 0)
     load.wait()
 
     low = iota((8, HALF), 0) < 4
@@ -216,6 +218,7 @@
     gram[...] = jnp.zeros_like(gram)
 
     def chunk(ch, carry):
+        here = pl.ds(pl.multiple_of(ch * W, W), W)
         finished(xm.at[ch, pl.ds(0, MAIN), :], own_main.at[ch])
         finished(xr.at[ch, 0], own_rest.at[ch])
         finished(xm.at[ch, pl.ds(0, (PEERS - 1) * MAIN), :], recv_main.at[ch])
@@ -232,15 +235,12 @@
             part = jnp.concatenate([xm[ch, s0 : s0 + KMAIN, :], xu[r0 : r0 + KREST, :]], axis=0)
             rows = jnp.dot(tab[b], part, preferred_element_type=F32).astype(BF16)
             for g in range(GROUPS):
-                spec[ch, g, 16 * b : 16 * b + 16, :] = rows[16 * g : 16 * g + 16, :]
-        weight = w[:, pl.ds(pl.multiple_of(ch * W, W), W)]
+                spec[g, 16 * b : 16 * b + 16, here] = rows[16 * g : 16 * g + 16, :]
+        weight = w[:, here]
         for g in range(GROUPS):
-            s = spec[ch, g]
+            s = spec[g, :, here]
             weighted = (s.astype(F32) * weight).astype(BF16)
             gram[g] += lax.dot_general(s, weighted, NT, preferred_element_type=F32)
-        pltpu.make_async_copy(
-            spec.at[ch], s_out.at[:, :, pl.ds(pl.multiple_of(ch * W, W), W)], out_sem.at[ch]
-        ).start()
         return carry
 
     lax.fori_loop(0, CHUNKS, chunk, 0)
@@ -327,30 +327,41 @@
     for ch in range(CHUNKS):
         finished(xm.at[ch, pl.ds(0, (PEERS - 1) * MAIN), :], send_main.at[ch])
         finished(xr.at[ch, pl.ds(0, PEERS - 1)], send_rest.at[ch])
-        pltpu.make_async_copy(
-            spec.at[ch], s_out.at[:, :, pl.ds(ch * W, W)], out_sem.at[ch]
-        ).wait()
-
-
-def project_kernel(hc, s, w, out):
-    h = hc[0].astype(F32)
+
+
+def project_kernel(hc, s, w, out, fields, sem):
     even = first_part((1, SIDE))
-    rows = jnp.concatenate(
-        [
-            jnp.where(even, h, -h),
-            jnp.where(even, pltpu.roll(h, SIDE - 1, 1), pltpu.roll(h, 1, 1)),
-        ],
-        axis=0,
-    ).astype(BF16)
-    coefs = jnp.dot(spread().astype(F32).astype(BF16), rows, preferred_element_type=F32)
-    coefs = jnp.where(same_frequency(), coefs, 0.0).astype(BF16)
+    expand = spread().astype(F32).astype(BF16)
+    mask = same_frequency()
     row, col = iota((SIDE, SIDE), 0), iota((SIDE, SIDE), 1)
     order = jnp.where(
         col == (row % 16) * 16 + (row // 32) * 2 + (row // 16) % 2, 1.0, 0.0
     ).astype(BF16)
-    matrix = lax.dot_general(order, coefs, NT, preferred_element_type=F32).astype(BF16)
-    field = jnp.dot(matrix, s[0], preferred_element_type=F32)
-    out[...] = (field * jnp.sqrt(w[...])).astype(BF16)
+    root = jnp.sqrt(w[...])
+    copies = []
+    for g in range(GROUPS):
+        h = hc[g].astype(F32)
+        rows = jnp.concatenate(
+            [
+                jnp.where(even, h, -h),
+                jnp.where(even, pltpu.roll(h, SIDE - 1, 1), pltpu.roll(h, 1, 1)),
+            ],
+            axis=0,
+        ).astype(BF16)
+        coefs = jnp.dot(expand, rows, preferred_element_type=F32)
+        coefs = jnp.where(mask, coefs, 0.0).astype(BF16)
+        count = min(SIDE, (FREQS - g * GROUP) * 2 * BLOCKS)
+        matrix = lax.dot_general(order[:count], coefs, NT, preferred_element_type=F32)
+        field = jnp.dot(matrix.astype(BF16), s[g], preferred_element_type=F32)
+        fields[g, :count] = (field * root).astype(BF16)
+        copies.append(
+            pltpu.make_async_copy(
+                fields.at[g, pl.ds(0, count)], out.at[pl.ds(g * SIDE, count)], sem.at[g]
+            )
+        )
+        copies[-1].start()
+    for copy in copies:
+        copy.wait()
 
 
 def shards(snapshots, weights, freq_ids, starts):
@@ -361,11 +372,11 @@
         spectra_kernel,
         name="exchange_spectra",
         out_shape=(
-            jax.ShapeDtypeStruct((GROUPS, SIDE, POINTS), BF16),
-            jax.ShapeDtypeStruct((GROUPS, BLOCKS, SIDE), BF16),
+            pltpu.VMEM((GROUPS, SIDE, POINTS), BF16),
+            pltpu.VMEM((GROUPS, BLOCKS, SIDE), BF16),
         ),
         in_specs=[anywhere, vmem, vmem, pl.BlockSpec(memory_space=pltpu.SMEM)],
-        out_specs=(anywhere, vmem),
+        out_specs=(vmem, vmem),
         scratch_shapes=[
             pltpu.VMEM((ROWS, PEERS * POINTS), BF16),
             pltpu.VMEM((PEERS, CHUNKS, 8, HALF), BF16),
@@ -373,7 +384,6 @@
             pltpu.VMEM((CHUNKS, PEERS, 8, HALF), BF16),
             pltpu.VMEM((PEERS * REST, W), BF16),
             pltpu.VMEM((BLOCKS, TROWS, KMAIN + KREST), BF16),
-            pltpu.VMEM((CHUNKS, GROUPS, SIDE, W), BF16),
             pltpu.VMEM((GROUPS, SIDE, SIDE), F32),
             pltpu.VMEM((GROUPS, BLOCKS, SIDE), F32),
             pltpu.VMEM((16, BLOCKS, SIDE), F32),
@@ -382,7 +392,7 @@
             pltpu.VMEM((BLOCKS, SIDE), BF16),
             pltpu.VMEM((2, 2, BLOCKS * 8, 128), F32),
             dma(()), dma((CHUNKS,)), dma((CHUNKS,)), dma((CHUNKS,)), dma((CHUNKS,)),
-            dma((CHUNKS,)), dma((CHUNKS,)), dma((CHUNKS,)),
+            dma((CHUNKS,)), dma((CHUNKS,)),
             dma((GROUPS,)), dma(()), dma(()), dma(()), dma(()), dma((GROUPS,)),
         ],
         compiler_params=pltpu.CompilerParams(
@@ -392,14 +402,11 @@
     field = pl.pallas_call(
         project_kernel,
         name="project_modes",
-        grid=(GROUPS,),
         out_shape=jax.ShapeDtypeStruct((FREQS * 2 * BLOCKS, POINTS), BF16),
-        in_specs=[
-            pl.BlockSpec((1, BLOCKS, SIDE), lambda g: (g, 0, 0)),
-            pl.BlockSpec((1, SIDE, POINTS), lambda g: (g, 0, 0)),
-            pl.BlockSpec((1, POINTS), lambda g: (0, 0)),
-        ],
-        out_specs=pl.BlockSpec((SIDE, POINTS), lambda g: (g, 0)),
+        in_specs=[vmem, vmem, vmem],
+        out_specs=anywhere,
+        scratch_shapes=[pltpu.VMEM((GROUPS, SIDE, POINTS), BF16), dma((GROUPS,))],
+        compiler_params=pltpu.CompilerParams(vmem_limit_bytes=24 << 20),
     )(coefs, spectra, weights)
     return field.reshape(FREQS, 2, BLOCKS, 1, POINTS)
 

time: 155 us -> 146 us (0.942)
  Pallas kernels: 155 us -> 146 us
    pallas_call x2, Pallas kernels: 155 us -> 146 us  [the longest x1 141 us: shards(): pl.pallas_call(spectra_kernel, name='exchange_spectra', out_shape=(pltpu....]
where the time goes in v2:
time: 146 us
  Pallas kernels  146 us (100%)
    pallas_call x1, Pallas kernels, shards(): pl.pallas_call(spectra_kernel, name='exchange_spectra', out_shape=(pltpu....  141 us
    pallas_call x1, Pallas kernels, shards(): pl.pallas_call(project_kernel, name='project_modes', out_shape=jax.ShapeD...  4.98 us

profile of v2, /device:TPU:1, one launch (start us, length us, event | category | flops | bytes accessed | tf_op | source)
XLA Modules:
  0.0 145.8 jit_solution(6902177420689000043)
XLA Ops:
  0.0 0.0 copy-start
  0.0 140.8 %exchange_spectra.1 = (bf16[9,256,1024]{2,1,0:T(8,128)(2,1)S(1)}, bf16[9,16,256]{2,1,0:T(8,128)(2,1)S(1)}) custom-call(bf16[36,65536]{1,0:T(8,128)(2,1)} %bitcast.5, f32[1,1024]{1,0:T(1,128)} %w.3, s32[1,65]{1,0:T(1,128)} %bitcast.6, s32[16]{0:T(128)} %starts.1), custom_call_target="tpu_custom_call" | custom-call | tf_op jit(solution)/shard_map/exchange_spectra/pallas_call | solution.py:371
  140.9 0.0 copy-done
  140.9 5.0 %project_modes.1 = bf16[2080,1024]{1,0:T(8,128)(2,1)} custom-call(bf16[9,16,256]{2,1,0:T(8,128)(2,1)S(1)} %get-tuple-element.7.hc, bf16[9,256,1024]{2,1,0:T(8,128)(2,1)S(1)} %get-tuple-element.8.s, f32[1,1024]{1,0:T(1,128)S(1)} %copy-done), custom_call_target="tpu_custom_call" | custom-call | tf_op jit(solution)/shard_map/project_modes/pallas_call | solution.py:402
Async XLA Ops:
  0.0 140.9 %copy-start = (f32[1,1024]{1,0:T(1,128)S(1)}, f32[1,1024]{1,0:T(1,128)}, u32[]{:S(2)}) copy-start(f32[1,1024]{1,0:T(1,128)} %w.3) | copy-start | bytes 12292

commit v3 on v2

--- a/solution.py
+++ b/solution.py
@@ -33,7 +33,6 @@
 MESH = pl.DeviceIdType.MESH
 F32 = jnp.float32
 BF16 = jnp.bfloat16
-HIGH = lax.Precision.HIGHEST
 NT = (((1,), (1,)), ((), ()))
 
 
@@ -95,6 +94,29 @@
     rest = col - KMAIN
     rest = ROWS * (first_rest(b) // REST + rest // REST) + MAIN + rest % REST
     return jnp.where(col < KMAIN, main, rest)
+
+
+def halves(m):
+    high = m.astype(BF16)
+    return high, (m - high.astype(F32)).astype(BF16)
+
+
+def product(a, b):
+    dot = functools.partial(jnp.dot, preferred_element_type=F32)
+    return dot(a[0], b[0]) + (dot(a[0], b[1]) + dot(a[1], b[0]))
+
+
+def fold(h):
+    h = h[:, :128] + pltpu.roll(h[:, 128:], 2, 1)
+    return h[:8] + pltpu.roll(h[8:], 4, 1)
+
+
+def unfold(q):
+    h = jnp.concatenate([q, pltpu.roll(q, 124, 1)], axis=0)
+    keep = iota((BLOCKS, 128), 1) % 16 < 2
+    return jnp.concatenate(
+        [jnp.where(keep, h, 0.0), jnp.where(keep, pltpu.roll(h, 126, 1), 0.0)], axis=1
+    )
 
 
 def solve_roots(h, group, h3):
@@ -114,22 +136,25 @@
         ],
         axis=0,
     )
-    mask = same_frequency()
-    dot = functools.partial(jnp.dot, precision=HIGH, preferred_element_type=F32)
-    approx = jnp.where(mask, dot(spread().astype(F32), rows / trace), 0.0)
+    rows = halves(rows / trace)
+    pick = spread().astype(F32).astype(BF16)
+    approx = sum(jnp.dot(pick, part, preferred_element_type=F32) for part in rows)
+    approx = jnp.where(same_frequency(), approx, 0.0)
     eye = jnp.where(iota((SIDE, SIDE), 0) == iota((SIDE, SIDE), 1), 1.5, 0.0)
     update = eye - 0.5 * approx
-    root = update
-    for _ in range(1, ITERS):
-        approx = dot(approx, update)
-        update = eye - 0.5 * dot(root, approx)
-        root = dot(update, root)
+    root, approx, update = halves(update), halves(approx), halves(update)
+    for step in range(1, ITERS):
+        approx = halves(product(approx, update))
+        update = halves(eye - 0.5 * product(root, approx))
+        root = product(update, root)
+        if step < ITERS - 1:
+            root = halves(root)
     return (first_rows(sum_frequencies(root), h3) * (1.0 / jnp.sqrt(trace))).astype(BF16)
 
 
 def spectra_kernel(
-    x, w, fid, starts, spec, hc,
-    xs, pk, xm, xr, xu, tab, gram, hsend, r1, h2, r2, hcs, h3,
+    x, w, fid, starts, spec, hc, expand, same, order, root,
+    xs, pk, xm, xr, xu, tab, gram, hsend, r1, h2, r2, h8, r18, h28, r28, solved, hcs, h3,
     in_sem, own_main, own_rest, send_main, send_rest, recv_main, recv_rest,
     s1_send, s1_recv, s2_send, s2_recv, s3_send, s3_recv,
 ):
@@ -152,20 +177,16 @@
 
     barrier = pltpu.get_barrier_semaphore()
 
-    def greet(k, carry):
-        pl.semaphore_signal(barrier, inc=1, device_id=plane(k), device_id_type=MESH)
-        return carry
-
-    def greet_far(k, carry):
+    ys, zs = [lax.rem(y + d, NY) for d in range(NY)], [lax.rem(z + d, NZ) for d in range(NZ)]
+    cs, xxs = [c, 1 - c], [lax.rem(xx + d, NX) for d in range(NX)]
+    steps = [(0, k // 16, k // 2 % 8, k % 2) for k in range(1, PEERS)]
+    steps += [(1 + k // 4, k % 4, 0, 0) for k in range(12)]
+    sizes = (NX, NY, NZ, NC)
+    for dx, dy, dz, dc in sorted(steps, key=lambda d: -sum(min(i, n - i) for i, n in zip(d, sizes))):
         pl.semaphore_signal(
-            barrier, inc=1, device_id=at(1 + k // 4, k % 4, 0, 0), device_id_type=MESH
-        )
-        return carry
-
-    for k in range(12):
-        greet_far(k, 0)
-    for k in range(PEERS - 1, 0, -1):
-        greet(k, 0)
+            barrier, inc=1, device_id_type=MESH,
+            device_id={"pts_0": ys[dy], "pts_1": zs[dz], "pts_2": cs[dc], "frq": xxs[dx]},
+        )
     load.wait()
 
     low = iota((8, HALF), 0) < 4
@@ -216,6 +237,13 @@
         pltpu.make_async_copy(ref, ref, sem).wait()
 
     gram[...] = jnp.zeros_like(gram)
+    expand[...] = spread().astype(F32).astype(BF16)
+    row, col = iota((SIDE, SIDE), 0), iota((SIDE, SIDE), 1)
+    same[...] = jnp.where(row // 32 == (col // 2) % GROUP, 1.0, 0.0)
+    order[...] = jnp.where(
+        row == (col % 16) * 16 + (col // 32) * 2 + (col // 16) % 2, 1.0, 0.0
+    ).astype(BF16)
+    root[...] = jnp.sqrt(w[...])
 
     def chunk(ch, carry):
         here = pl.ds(pl.multiple_of(ch * W, W), W)
@@ -245,38 +273,62 @@
 
     lax.fori_loop(0, CHUNKS, chunk, 0)
 
+    mine = jnp.where(c == 0, z, GROUPS - 1)
+    large = c == 0
+    small = (c == 1) & (z == 0)
+    here = z * NC + c
+    there = xx * NY + y
+
+    def stage1(g):
+        oz, oc = (g, 0) if g < NZ else (0, 1)
+        return pltpu.make_async_remote_copy(
+            src_ref=hsend.at[g] if g < NZ else h8, dst_ref=(r1 if g < NZ else r18).at[here],
+            send_sem=s1_send.at[g], recv_sem=s1_recv,
+            device_id={"pts_0": y, "pts_1": oz, "pts_2": oc, "frq": xx}, device_id_type=MESH,
+        )
+
+    def elsewhere(g):
+        return (z != g) | (c != 0) if g < NZ else (z != 0) | (c != 1)
+
+    def begin1(g):
+        @pl.when(elsewhere(g))
+        def _():
+            stage1(g).start()
+
     mask = same_frequency()
     even3 = first_part((BLOCKS, 8, SIDE))
-    for g in range(GROUPS):
+    for g in reversed(range(GROUPS)):
         m = sum_frequencies(jnp.where(mask, gram[g], 0.0))
         other = pltpu.roll(m, 7, 1)
         m = jnp.where(even3, m + pltpu.roll(other, SIDE - 1, 2), m - pltpu.roll(other, 1, 2))
-        hsend[g] = first_rows(m, h3.at[g % 2]) * (1.0 / TOTAL)
-
-    mine = jnp.where(c == 0, z, GROUPS - 1)
-    owner = (c == 0) | (z == 0)
-    here = z * NC + c
-
-    def stage1(g):
-        oz, oc = (g, 0) if g < NZ else (0, 1)
+        m = first_rows(m, h3.at[g % 2]) * (1.0 / TOTAL)
+        if g < NZ:
+            hsend[g] = m
+            begin1(g + 1)
+        else:
+            h8[...] = fold(m)
+    begin1(0)
+
+    def stage2(k, src, dst):
         return pltpu.make_async_remote_copy(
-            src_ref=hsend.at[g], dst_ref=r1.at[here], send_sem=s1_send.at[g], recv_sem=s1_recv,
-            device_id={"pts_0": y, "pts_1": oz, "pts_2": oc, "frq": xx}, device_id_type=MESH,
-        )
-
-    def elsewhere(g):
-        return (z != g) | (c != 0) if g < NZ else (z != 0) | (c != 1)
-
-    for g in range(GROUPS):
-        @pl.when(elsewhere(g))
-        def _():
-            stage1(g).start()
-
-    def stage2(k):
-        return pltpu.make_async_remote_copy(
-            src_ref=h2, dst_ref=r2.at[xx * NY + y], send_sem=s2_send, recv_sem=s2_recv,
+            src_ref=src, dst_ref=dst.at[there], send_sem=s2_send, recv_sem=s2_recv,
             device_id=at(k // 4, k % 4, 0, 0), device_id_type=MESH,
         )
+
+    def reduced(own, first, total, second):
+        first[here] = own
+        finished(first.at[pl.ds(0, 15)], s1_recv)
+        total[...] = sum((first[i] for i in range(1, 16)), first[0])
+        second[there] = total[...]
+
+        def send(k, carry):
+            stage2(k, total, second).start()
+            return carry
+
+        lax.fori_loop(1, 16, send, 0)
+        finished(second.at[pl.ds(0, 15)], s2_recv)
+        finished(second.at[pl.ds(0, 15)], s2_send)
+        return sum((second[i] for i in range(1, 16)), second[0])
 
     def stage3(k):
         return pltpu.make_async_remote_copy(
@@ -284,26 +336,17 @@
             device_id=at(0, 0, k // 2, k % 2), device_id_type=MESH,
         )
 
-    @pl.when(owner)
+    @pl.when(large)
     def _():
-        r1[here] = hsend[mine]
-        finished(r1.at[pl.ds(0, 15)], s1_recv)
-        total = r1[0]
-        for i in range(1, 16):
-            total = total + r1[i]
-        h2[...] = total
-        r2[xx * NY + y] = total
-
-        def out2(k, carry):
-            stage2(k).start()
-            return carry
-
-        lax.fori_loop(1, 16, out2, 0)
-        finished(r2.at[pl.ds(0, 15)], s2_recv)
-        total = r2[0]
-        for i in range(1, 16):
-            total = total + r2[i]
-        coefs = solve_roots(total, mine, h3.at[0])
+        solved[...] = reduced(hsend[z], r1, h2, r2)
+
+    @pl.when(small)
+    def _():
+        solved[...] = unfold(reduced(h8[...], r18, h28, r28))
+
+    @pl.when(large | small)
+    def _():
+        coefs = solve_roots(solved[...], mine, h3.at[0])
         hcs[...] = coefs
         hc[mine] = coefs
 
@@ -312,7 +355,6 @@
             return carry
 
         lax.fori_loop(1, 16, out3, 0)
-        finished(r2.at[pl.ds(0, 15)], s2_send)
 
     for g in range(GROUPS):
         @pl.when(elsewhere(g))
@@ -320,7 +362,7 @@
             stage1(g).wait_send()
             finished(hc.at[g], s3_recv.at[g])
 
-    @pl.when(owner)
+    @pl.when(large | small)
     def _():
         finished(xm.at[0, pl.ds(0, 15 * BLOCKS), :], s3_send)
 
@@ -329,31 +371,28 @@
         finished(xr.at[ch, pl.ds(0, PEERS - 1)], send_rest.at[ch])
 
 
-def project_kernel(hc, s, w, out, fields, sem):
-    even = first_part((1, SIDE))
-    expand = spread().astype(F32).astype(BF16)
-    mask = same_frequency()
-    row, col = iota((SIDE, SIDE), 0), iota((SIDE, SIDE), 1)
-    order = jnp.where(
-        col == (row % 16) * 16 + (row // 32) * 2 + (row // 16) % 2, 1.0, 0.0
-    ).astype(BF16)
-    root = jnp.sqrt(w[...])
-    copies = []
+def project_kernel(hc, s, expand, same, order, root, out, fields, matrices, sem):
+    coefs = hc[...].astype(F32).reshape(GROUPS * BLOCKS, SIDE).astype(BF16)
+    coefs = jnp.dot(coefs, order[...], preferred_element_type=F32)
+    real = (iota((1, SIDE), 1) // BLOCKS) % 2 == 0
     for g in range(GROUPS):
-        h = hc[g].astype(F32)
+        h = coefs[BLOCKS * g : BLOCKS * (g + 1)]
         rows = jnp.concatenate(
             [
-                jnp.where(even, h, -h),
-                jnp.where(even, pltpu.roll(h, SIDE - 1, 1), pltpu.roll(h, 1, 1)),
+                jnp.where(real, h, -h),
+                jnp.where(real, pltpu.roll(h, SIDE - BLOCKS, 1), pltpu.roll(h, BLOCKS, 1)),
             ],
             axis=0,
         ).astype(BF16)
-        coefs = jnp.dot(expand, rows, preferred_element_type=F32)
-        coefs = jnp.where(mask, coefs, 0.0).astype(BF16)
+        matrix = lax.dot_general(
+            rows, expand[...], (((0,), (1,)), ((), ())), preferred_element_type=F32
+        )
+        matrices[g] = (matrix * same[...]).astype(BF16)
+    copies = []
+    for g in range(GROUPS):
         count = min(SIDE, (FREQS - g * GROUP) * 2 * BLOCKS)
-        matrix = lax.dot_general(order[:count], coefs, NT, preferred_element_type=F32)
-        field = jnp.dot(matrix.astype(BF16), s[g], preferred_element_type=F32)
-        fields[g, :count] = (field * root).astype(BF16)
+        field = jnp.dot(matrices[g, :count, :], s[g], preferred_element_type=F32)
+        fields[g, :count] = (field * root[...]).astype(BF16)
         copies.append(
             pltpu.make_async_copy(
                 fields.at[g, pl.ds(0, count)], out.at[pl.ds(g * SIDE, count)], sem.at[g]
@@ -368,15 +407,19 @@
     vmem = pl.BlockSpec(memory_space=pltpu.VMEM)
     anywhere = pl.BlockSpec(memory_space=pl.ANY)
     dma = pltpu.SemaphoreType.DMA
-    spectra, coefs = pl.pallas_call(
+    spectra, coefs, *shared = pl.pallas_call(
         spectra_kernel,
         name="exchange_spectra",
         out_shape=(
             pltpu.VMEM((GROUPS, SIDE, POINTS), BF16),
             pltpu.VMEM((GROUPS, BLOCKS, SIDE), BF16),
+            pltpu.VMEM((SIDE, 2 * BLOCKS), BF16),
+            pltpu.VMEM((SIDE, SIDE), F32),
+            pltpu.VMEM((SIDE, SIDE), BF16),
+            pltpu.VMEM((1, POINTS), F32),
         ),
         in_specs=[anywhere, vmem, vmem, pl.BlockSpec(memory_space=pltpu.SMEM)],
-        out_specs=(vmem, vmem),
+        out_specs=(vmem,) * 6,
         scratch_shapes=[
             pltpu.VMEM((ROWS, PEERS * POINTS), BF16),
             pltpu.VMEM((PEERS, CHUNKS, 8, HALF), BF16),
@@ -385,10 +428,15 @@
             pltpu.VMEM((PEERS * REST, W), BF16),
             pltpu.VMEM((BLOCKS, TROWS, KMAIN + KREST), BF16),
             pltpu.VMEM((GROUPS, SIDE, SIDE), F32),
-            pltpu.VMEM((GROUPS, BLOCKS, SIDE), F32),
+            pltpu.VMEM((NZ, BLOCKS, SIDE), F32),
             pltpu.VMEM((16, BLOCKS, SIDE), F32),
             pltpu.VMEM((BLOCKS, SIDE), F32),
             pltpu.VMEM((16, BLOCKS, SIDE), F32),
+            pltpu.VMEM((8, 128), F32),
+            pltpu.VMEM((16, 8, 128), F32),
+            pltpu.VMEM((8, 128), F32),
+            pltpu.VMEM((16, 8, 128), F32),
+            pltpu.VMEM((BLOCKS, SIDE), F32),
             pltpu.VMEM((BLOCKS, SIDE), BF16),
             pltpu.VMEM((2, 2, BLOCKS * 8, 128), F32),
             dma(()), dma((CHUNKS,)), dma((CHUNKS,)), dma((CHUNKS,)), dma((CHUNKS,)),
@@ -403,11 +451,15 @@
         project_kernel,
         name="project_modes",
         out_shape=jax.ShapeDtypeStruct((FREQS * 2 * BLOCKS, POINTS), BF16),
-        in_specs=[vmem, vmem, vmem],
+        in_specs=[vmem] * 6,
         out_specs=anywhere,
-        scratch_shapes=[pltpu.VMEM((GROUPS, SIDE, POINTS), BF16), dma((GROUPS,))],
+        scratch_shapes=[
+            pltpu.VMEM((GROUPS, SIDE, POINTS), BF16),
+            pltpu.VMEM((GROUPS, SIDE, SIDE), BF16),
+            dma((GROUPS,)),
+        ],
         compiler_params=pltpu.CompilerParams(vmem_limit_bytes=24 << 20),
-    )(coefs, spectra, weights)
+    )(coefs, spectra, *shared)
     return field.reshape(FREQS, 2, BLOCKS, 1, POINTS)
 
 

time: 146 us -> 142 us (0.973)
  Pallas kernels: 146 us -> 142 us
    pallas_call x1, Pallas kernels: 4.98 us -> 3.03 us  [shards(): pl.pallas_call(project_kernel, name='project_modes', out_shape=jax.ShapeD...]
    pallas_call x1, Pallas kernels: 141 us -> 139 us  [shards(): pl.pallas_call(spectra_kernel, name='exchange_spectra', out_shape=(pltpu....]
where the time goes in v3:
time: 142 us
  Pallas kernels  142 us (100%)
    pallas_call x1, Pallas kernels, shards(): pl.pallas_call(spectra_kernel, name='exchange_spectra', out_shape=(pltpu....  139 us
    pallas_call x1, Pallas kernels, shards(): pl.pallas_call(project_kernel, name='project_modes', out_shape=jax.ShapeD...  3.03 us

profile of v3, /device:TPU:1, one launch (start us, length us, event | category | flops | bytes accessed | tf_op | source)
XLA Modules:
  0.0 142.1 jit_solution(1310577939925678174)
XLA Ops:
  0.0 139.1 %exchange_spectra.1 = (bf16[9,256,1024]{2,1,0:T(8,128)(2,1)S(1)}, bf16[9,16,256]{2,1,0:T(8,128)(2,1)S(1)}, bf16[256,32]{1,0:T(8,128)(2,1)S(1)}, f32[256,256]{1,0...) custom-call(bf16[36,65536]{1,0:T(8,128)(2,1)} %bitcast.5, f32[1,1024]{1,0:T(1,128)} %w.1, ...), custom_call_target="tpu_custom_call" | custom-call | tf_op jit(solution)/shard_map/exchange_spectra/pallas_call | solution.py:410
  139.1 3.0 %project_modes.1 = bf16[2080,1024]{1,0:T(8,128)(2,1)} custom-call(bf16[9,16,256]{2,1,0:T(8,128)(2,1)S(1)} %get-tuple-element.11.hc, bf16[9,256,1024]{2,1,0:T(8,128)(2,1)S(1)} %get-tuple-element.12.s, bf16[256,32]{1,0:T(8,128)(2,1)S(1)} %get-tuple-element.13.expand, f32[256,256]{1,0:T(8,128)S(1)} %get-tuple-element.14.same, ...), custom_call_target="tpu_custom_call" | custom-call | tf_op jit(solution)/shard_map/project_modes/pallas_call | solution.py:450

commit v4 on v3

--- a/solution.py
+++ b/solution.py
@@ -94,6 +94,13 @@
     rest = col - KMAIN
     rest = ROWS * (first_rest(b) // REST + rest // REST) + MAIN + rest % REST
     return jnp.where(col < KMAIN, main, rest)
+
+
+def far_first(sizes):
+    def distance(k):
+        return sum(min(i, n - i) for i, n in zip((k // sizes[1], k % sizes[1]), sizes))
+
+    return sorted(range(1, sizes[0] * sizes[1]), key=lambda k: -distance(k))
 
 
 def halves(m):
@@ -153,9 +160,9 @@
 
 
 def spectra_kernel(
-    x, w, fid, starts, spec, hc, expand, same, order, root,
-    xs, pk, xm, xr, xu, tab, gram, hsend, r1, h2, r2, h8, r18, h28, r28, solved, hcs, h3,
-    in_sem, own_main, own_rest, send_main, send_rest, recv_main, recv_rest,
+    x, w_in, fid_in, starts, spec, hc, expand, same, order, root,
+    xs, pk, xm, xr, xu, tab, gram, hsend, r1, h2, r2, h8, r18, h28, r28, solved, hcs, h3, w, fid,
+    in_sem, small_sem, own_main, own_rest, send_main, send_rest, recv_main, recv_rest,
     s1_send, s1_recv, s2_send, s2_recv, s3_send, s3_recv,
 ):
     y, z, c = (lax.axis_index(a) for a in PTS)
@@ -163,6 +170,12 @@
     me = (y * NZ + z) * NC + c
     load = pltpu.make_async_copy(x, xs, in_sem)
     load.start()
+    small_loads = [
+        pltpu.make_async_copy(w_in, w, small_sem.at[0]),
+        pltpu.make_async_copy(fid_in, fid, small_sem.at[1]),
+    ]
+    for copy in small_loads:
+        copy.start()
 
     def at(dx, dy, dz, dc):
         return {
@@ -227,6 +240,8 @@
 
         lax.fori_loop(1, PEERS, send, 0)
 
+    for copy in small_loads:
+        copy.wait()
     table = make_table(fid[...])
     tau = iota((NFFT, KMAIN + KREST), 0)
     for b in range(BLOCKS):
@@ -312,7 +327,10 @@
     def stage2(k, src, dst):
         return pltpu.make_async_remote_copy(
             src_ref=src, dst_ref=dst.at[there], send_sem=s2_send, recv_sem=s2_recv,
-            device_id=at(k // 4, k % 4, 0, 0), device_id_type=MESH,
+            device_id={
+                "pts_0": ys[k % 4], "pts_1": z, "pts_2": c, "frq": xxs[k // 4],
+            },
+            device_id_type=MESH,
         )
 
     def reduced(own, first, total, second):
@@ -321,19 +339,18 @@
         total[...] = sum((first[i] for i in range(1, 16)), first[0])
         second[there] = total[...]
 
-        def send(k, carry):
+        for k in far_first((NX, NY)):
             stage2(k, total, second).start()
-            return carry
-
-        lax.fori_loop(1, 16, send, 0)
         finished(second.at[pl.ds(0, 15)], s2_recv)
+        result = sum((second[i] for i in range(1, 16)), second[0])
         finished(second.at[pl.ds(0, 15)], s2_send)
-        return sum((second[i] for i in range(1, 16)), second[0])
+        return result
 
     def stage3(k):
         return pltpu.make_async_remote_copy(
             src_ref=hcs, dst_ref=hc.at[mine], send_sem=s3_send, recv_sem=s3_recv.at[mine],
-            device_id=at(0, 0, k // 2, k % 2), device_id_type=MESH,
+            device_id={"pts_0": y, "pts_1": zs[k // 2], "pts_2": cs[k % 2], "frq": xx},
+            device_id_type=MESH,
         )
 
     @pl.when(large)
@@ -350,11 +367,8 @@
         hcs[...] = coefs
         hc[mine] = coefs
 
-        def out3(k, carry):
+        for k in far_first((NZ, NC)):
             stage3(k).start()
-            return carry
-
-        lax.fori_loop(1, 16, out3, 0)
 
     for g in range(GROUPS):
         @pl.when(elsewhere(g))
@@ -418,7 +432,7 @@
             pltpu.VMEM((SIDE, SIDE), BF16),
             pltpu.VMEM((1, POINTS), F32),
         ),
-        in_specs=[anywhere, vmem, vmem, pl.BlockSpec(memory_space=pltpu.SMEM)],
+        in_specs=[anywhere, anywhere, anywhere, pl.BlockSpec(memory_space=pltpu.SMEM)],
         out_specs=(vmem,) * 6,
         scratch_shapes=[
             pltpu.VMEM((ROWS, PEERS * POINTS), BF16),
@@ -439,7 +453,9 @@
             pltpu.VMEM((BLOCKS, SIDE), F32),
             pltpu.VMEM((BLOCKS, SIDE), BF16),
             pltpu.VMEM((2, 2, BLOCKS * 8, 128), F32),
-            dma(()), dma((CHUNKS,)), dma((CHUNKS,)), dma((CHUNKS,)), dma((CHUNKS,)),
+            pltpu.VMEM((1, POINTS), F32),
+            pltpu.VMEM((1, FREQS), jnp.int32),
+            dma(()), dma((2,)), dma((CHUNKS,)), dma((CHUNKS,)), dma((CHUNKS,)), dma((CHUNKS,)),
             dma((CHUNKS,)), dma((CHUNKS,)),
             dma((GROUPS,)), dma(()), dma(()), dma(()), dma(()), dma((GROUPS,)),
         ],

time: 142 us -> 141 us (level)
  no operation moved by 1% of the time
where the time goes in v4:
time: 141 us
  Pallas kernels  141 us (100%)
    pallas_call x1, Pallas kernels, shards(): pl.pallas_call(spectra_kernel, name='exchange_spectra', out_shape=(pltpu....  138 us
    pallas_call x1, Pallas kernels, shards(): pl.pallas_call(project_kernel, name='project_modes', out_shape=jax.ShapeD...  3.03 us

profile of v4, /device:TPU:1, one launch (start us, length us, event | category | flops | bytes accessed | tf_op | source)
XLA Modules:
  0.0 140.9 jit_solution(8939752557998915244)
XLA Ops:
  0.0 137.8 %exchange_spectra.1 = (bf16[9,256,1024]{2,1,0:T(8,128)(2,1)S(1)}, bf16[9,16,256]{2,1,0:T(8,128)(2,1)S(1)}, bf16[256,32]{1,0:T(8,128)(2,1)S(1)}, f32[256,256]{1,0...) custom-call(bf16[36,65536]{1,0:T(8,128)(2,1)} %bitcast.5, f32[1,1024]{1,0:T(1,128)} %w_in.1, ...), custom_call_target="tpu_custom_call" | custom-call | tf_op jit(solution)/shard_map/exchange_spectra/pallas_call | solution.py:424
  137.8 3.0 %project_modes.1 = bf16[2080,1024]{1,0:T(8,128)(2,1)} custom-call(bf16[9,16,256]{2,1,0:T(8,128)(2,1)S(1)} %get-tuple-element.11.hc, bf16[9,256,1024]{2,1,0:T(8,128)(2,1)S(1)} %get-tuple-element.12.s, bf16[256,32]{1,0:T(8,128)(2,1)S(1)} %get-tuple-element.13.expand, f32[256,256]{1,0:T(8,128)S(1)} %get-tuple-element.14.same, ...), custom_call_target="tpu_custom_call" | custom-call | tf_op jit(solution)/shard_map/project_modes/pallas_call | solution.py:466
